TPU v7x, 256 devices: a whole 4x4x8 slice. The times are simulated.
256 devices in a mesh: shot: 16 (over z_hi, y, core), dom: 16 (over x, z_lo).
Axes of the slice: x: 4, y: 4, z: 8 (z_hi: 2, z_lo: 4; z = z_hi * 4 + z_lo), core: 2. Of those that a mesh axis runs over, the one named last changes fastest.
Arguments:
- model_slab: float32 [256, 128, 128], P('dom'), may hold values from 0.0225 to 0.17
- wave_prev: float32 [16, 256, 128, 128], P('shot', 'dom'), may hold values from -6 to 6
- wave_now: float32 [16, 256, 128, 128], P('shot', 'dom'), may hold values from -6 to 6
- adjoint_next: float32 [16, 256, 128, 128], P('shot', 'dom'), may hold values from -6 to 6
- adjoint_now: float32 [16, 256, 128, 128], P('shot', 'dom'), may hold values from -6 to 6
- wavelet: float32 [16, 8], P('shot'), may hold values from -12 to 12
- source_cell: int32 [16], P('shot'), may hold values from 0 to 4194303
- receiver_cells: int32 [16, 256], P('shot'), may hold values from 0 to 4194303
- observed: float32 [16, 8, 256], P('shot'), may hold values from -6 to 6
Outputs:
- direction: float32 [256, 128, 128], P('dom')
- new_model: float32 [256, 128, 128], P('dom')
Inputs may be any that keep to these rules, and one draw needn't show every extreme that they name: `source_cell`: flat cell index x * 128 * 128 + y * 128 + z. `receiver_cells`: flat cell indices x * 128 * 128 + y * 128 + z; a cell may repeat.
All inputs are finite; a program needn't handle non-finite values. Where the computation divides by a largest or mean magnitude, that divisor is 1e-20 or more.
Results may differ from a plain program's by a relative error of at most 0.000025.
Values sent between devices are 32-bit elements; how exact they have to be, the bound alone decides.
No kernel may reach another device: no remote copies, remote signals or barrier semaphores. Data moves between devices by JAX's collectives and lax.ppermute only.
A program may use at most 192 MiB of HBM per device.

v0:
```python
import jax
import jax.numpy as jnp
from jax import lax
from jax.sharding import PartitionSpec as P

STEPS = 8
COEFFS = (8.0 / 5.0, -1.0 / 5.0, 8.0 / 315.0, -1.0 / 560.0)
CENTRE = -205.0 / 72.0
STEP_FRACTION = 0.1
EPSILON = 1e-06


def padded_2(cells, sides, width):
    for axis, dim in sides:
        count = lax.axis_size(axis)
        ends = count - 1
        head = lax.slice_in_dim(cells, 0, width, axis=dim)
        tail = lax.slice_in_dim(cells, cells.shape[dim] - width, cells.shape[dim], axis=dim)
        cells = jnp.concatenate(
            [
                lax.ppermute(tail, axis, [(i, (i + 1) % count) for i in range(ends)]),
                cells,
                lax.ppermute(head, axis, [((i + 1) % count, i) for i in range(ends)]),
            ],
            axis=dim,
        )
    return cells


def shifted(field, axis, offset):
    length = field.shape[axis]
    filler_shape = list(field.shape)
    filler_shape[axis] = abs(offset)
    filler = jnp.zeros(filler_shape, field.dtype)
    if offset > 0:
        return jnp.concatenate([lax.slice_in_dim(field, offset, length, axis=axis), filler], axis)
    return jnp.concatenate([filler, lax.slice_in_dim(field, 0, length + offset, axis=axis)], axis)


def laplace(padded):
    rows = padded.shape[0] - 8
    field = padded[4 : 4 + rows]
    total = 3.0 * CENTRE * field
    for index, weight in enumerate(COEFFS):
        offset = index + 1
        total = total + weight * (
            padded[4 + offset : 4 + offset + rows] + padded[4 - offset : 4 - offset + rows]
        )
    for axis in (1, 2):
        for index, weight in enumerate(COEFFS):
            offset = index + 1
            total = total + weight * (shifted(field, axis, offset) + shifted(field, axis, -offset))
    return total


def add_at(field, start_row, targets, amounts):
    count = field.size
    plane = field.shape[1] * field.shape[2]
    relative = targets - start_row * plane
    inside = (relative >= 0) & (relative < count)
    slots = jnp.clip(relative, 0, count - 1)
    values = jnp.where(inside, amounts, 0.0)
    return field.reshape(-1).at[slots].add(values).reshape(field.shape)


def on_device(
    model_slab,
    wave_prev,
    wave_now,
    adjoint_next,
    adjoint_now,
    wavelet,
    source_cell,
    receiver_cells,
    observed,
):
    shape = model_slab.shape
    rows = shape[0]
    cells = shape[0] * shape[1] * shape[2]
    own_row = lax.axis_index("dom") * rows
    first_cell = own_row * shape[1] * shape[2]
    source_one = source_cell[0]
    receivers = receiver_cells[0]
    receiver_local = receivers - first_cell
    receiver_inside = (receiver_local >= 0) & (receiver_local < cells)
    receiver_slots = jnp.clip(receiver_local, 0, cells - 1)
    images = []
    residuals = []
    gradient = jnp.zeros(shape, jnp.float32)
    older, current = (wave_prev[0], wave_now[0])
    for tick in range(STEPS):
        padded = padded_2(current, (("dom", 0),), 4)
        image = laplace(padded)
        newer = 2.0 * current - older + model_slab * image
        newer = add_at(newer, own_row, source_one, wavelet[0, tick])
        values = newer.reshape(-1)[receiver_slots] - observed[0, tick]
        residuals.append(jnp.where(receiver_inside, values, 0.0))
        images.append(image)
        older, current = (current, newer)
    later, present = (adjoint_next[0], adjoint_now[0])
    for tick in reversed(range(STEPS)):
        padded = padded_2(present, (("dom", 0),), 4)
        earlier = 2.0 * present - later + model_slab * laplace(padded)
        earlier = add_at(earlier, own_row, receivers, residuals[tick])
        gradient = gradient + earlier * images[tick]
        later, present = (present, earlier)
    total = lax.psum(gradient, "shot")
    peak = lax.pmax(jnp.max(jnp.abs(total)), "dom")
    direction = total / (peak + EPSILON)
    new_model = model_slab * (1.0 - STEP_FRACTION * direction)
    return (direction, new_model)


def solution(mesh):
    placed = (
        P("dom", None, None),
        P("shot", "dom", None, None),
        P("shot", "dom", None, None),
        P("shot", "dom", None, None),
        P("shot", "dom", None, None),
        P("shot", None),
        P("shot"),
        P("shot", None),
        P("shot", None, None),
    )
    return jax.shard_map(
        on_device,
        mesh=mesh,
        in_specs=placed,
        out_specs=(P("dom", None, None), P("dom", None, None)),
        check_vma=False,
    )
```

profile of v0, /device:TPU:0, one launch (start us, length us, event | category | flops | bytes accessed | tf_op | source)
XLA Modules:
  0.0 704.6 jit_solution(66041510398555331)
XLA Ops:
  54.4 9.5 %fusion.432 = (f32[16,128,128]{2,1,0:T(8,128)S(1)}, f32[16,128,128]{2,1,0:T(8,128)}) fusion(f32[1,16,128,128]{3,2,1,0:T(8,128)} %param.26, f32[16,128,128]{2,1,0:T(8,128)} %param.25, f32[1,16,128,128]{3,2,1,0:T(8,128)S(1)} %copy-done.9, f32[16,128,124]{2,1,0:T(8,128)} %get-tuple-element.385, f32[16,128,124]{2,1,0:T(8,128)} %get-tuple-element.384, ...), kind=kLoop, calls=%fused_computation.673 | loop fusion | flops 12845056 | bytes 23265280 | tf_op jit(solution)/shard_map/add | solution.py:94
  80.7 7.3 %fusion.388 = f32[16,128,128]{2,1,0:T(8,128)S(1)} fusion(f32[16,128,128]{2,1,0:T(8,128)S(1)} %copy-done.13, f32[16,128,128]{2,1,0:T(8,128)S(1)} %bitcast.275, f32[4,128,128]{2,1,0:T(8,128)} %collective-permute-done.1, f32[4,128,128]{2,1,0:T(8,128)S(1)} %collective-permute-done, f32[1,16,128,128]{3,2,1,0:T(8,128)} %param.28, ...), kind=kLoop, calls=%fused_computation.596 | loop fusion | flops 12845056 | bytes 21168128 | tf_op jit(solution)/shard_map/add | solution.py:103
  113.9 10.0 %collective-permute-done.6 = f32[4,128,128]{2,1,0:T(8,128)S(1)} collective-permute-done((f32[4,128,128]{2,1,0:T(8,128)S(1)}, f32[4,128,128]{2,1,0:T(8,128)S(1)}, u32[]{:S(2)}, u32[]{:S(2)}) %collective-permute-start.6) | collective-permute-done | bytes 262176 | tf_op jit(solution)/shard_map/ppermute | solution.py:23
  123.9 7.4 %multiply_add_fusion.6 = (f32[16,128,128]{2,1,0:T(8,128)S(1)}, f32[16,128,128]{2,1,0:T(8,128)}) fusion(f32[16,128,128]{2,1,0:T(8,128)S(1)} %copy-done.14, f32[16,128,128]{2,1,0:T(8,128)S(1)} %bitcast.225, f32[16,128,128]{2,1,0:T(8,128)} %bitcast.235, f32[16,128,124]{2,1,0:T(8,128)S(1)} %get-tuple-element.349, f32[16,128,124]{2,1,0:T(8,128)S(1)} %get-tuple-element.348, ...), kind=kLoop, calls=%fused_computation.683 | loop fusion | flops 12845056 | bytes 22216704 | tf_op jit(solution)/shard_map/add | solution.py:94
  144.2 9.8 %collective-permute-done.8 = f32[4,128,128]{2,1,0:T(8,128)S(1)} collective-permute-done((f32[4,128,128]{2,1,0:T(8,128)S(1)}, f32[4,128,128]{2,1,0:T(8,128)S(1)}, u32[]{:S(2)}, u32[]{:S(2)}) %collective-permute-start.8) | collective-permute-done | bytes 262176 | tf_op jit(solution)/shard_map/ppermute | solution.py:23
  171.3 9.9 %collective-permute-done.10 = f32[4,128,128]{2,1,0:T(8,128)S(1)} collective-permute-done((f32[4,128,128]{2,1,0:T(8,128)S(1)}, f32[4,128,128]{2,1,0:T(8,128)S(1)}, u32[]{:S(2)}, u32[]{:S(2)}) %collective-permute-start.10) | collective-permute-done | bytes 262176 | tf_op jit(solution)/shard_map/ppermute | solution.py:23
  188.2 10.4 %gather_fusion.3 = f32[256]{0:T(256)S(1)} fusion(f32[262144]{0:T(1024)} %fusion.437, s32[1024]{0:T(1024)S(1)} %pad_clamp_fusion), kind=kCustom, calls=%fused_computation.3 | custom fusion | bytes 3072 | tf_op jit(solution)/shard_map/gather | solution.py:96
  219.3 5.7 collective-permute-done.12
  225.0 7.6 %multiply_add_fusion.3 = (f32[16,128,128]{2,1,0:T(8,128)S(1)}, f32[16,128,128]{2,1,0:T(8,128)}) fusion(f32[16,128,128]{2,1,0:T(8,128)S(1)} %copy-done.17, f32[16,128,128]{2,1,0:T(8,128)S(1)} %bitcast.203, f32[16,128,128]{2,1,0:T(8,128)} %bitcast.40, f32[16,128,124]{2,1,0:T(8,128)S(1)} %get-tuple-element.295, f32[16,128,124]{2,1,0:T(8,128)S(1)} %get-tuple-element.294, ...), kind=kLoop, calls=%fused_computation.680 | loop fusion | flops 12845056 | bytes 22216704 | tf_op jit(solution)/shard_map/add | solution.py:94
  243.7 6.0 collective-permute-done.14
  265.9 6.4 collective-permute-done.16
  279.3 10.4 %gather_fusion = f32[256]{0:T(256)S(1)} fusion(f32[262144]{0:T(1024)} %fusion.440, s32[1024]{0:T(1024)S(1)} %pad_clamp_fusion), kind=kCustom, calls=%fused_computation | custom fusion | bytes 3072 | tf_op jit(solution)/shard_map/gather | solution.py:96
  320.8 6.2 collective-permute-done.20
  341.9 6.4 collective-permute-done.22
  367.3 6.6 collective-permute-done.24
  394.2 6.5 collective-permute-done.26
  400.7 5.7 fusion.66
  421.2 6.5 collective-permute-done.28
  427.7 5.7 fusion.40
  448.2 6.5 collective-permute-done.30
  454.7 5.8 fusion.14
  465.0 7.7 %multiply_add_fusion = f32[16,128,128]{2,1,0:T(8,128)} fusion(f32[16,128,128]{2,1,0:T(8,128)} %bitcast.277, f32[16,128,128]{2,1,0:T(8,128)} %get-tuple-element.115, f32[16,128,128]{2,1,0:T(8,128)} %bitcast.238, f32[16,128,128]{2,1,0:T(8,128)} %get-tuple-element.113, f32[16,128,128]{2,1,0:T(8,128)} %bitcast.171, f32[16,128,128]{2,1,0:T(8,128)} %get-tuple-element.111, ...), kind=kLoop, calls=%fused_computation.677 | loop fusion | flops 3932160 | bytes 17825792 | tf_op jit(solution)/shard_map/add | solution.py:105
  472.7 177.1 %all-reduce.258.cloned.1.call-done = f32[16,128,128]{2,1,0:T(8,128)} async-done(((f32[16,128,128]{2,1,0:T(8,128)}), f32[16,128,128]{2,1,0:T(8,128)}) %all-reduce.258.cloned.1.call-update) | async-done | bytes 1048592 | tf_op jit(solution)/shard_map/psum | solution.py:107
  651.8 43.5 %pmax.7 = f32[]{:T(128)} all-reduce(f32[]{:T(128)} %abs_reduce_fusion), channel_id=1, replica_groups=mesh['shot'=16,'dom'=16] {'dom'}, use_global_device_ids=true, to_apply=%region_10.11 | all-reduce | flops 1 | bytes 8 | tf_op jit(solution)/shard_map/pmax | solution.py:108
  (335 shorter events, 297.9 us)
Async XLA Ops:
  7.2 642.6 %all-reduce.258.cloned.1.call-start = ((), (), s32[]{:S(2)}) async-start(), calls=%async_computation | async-start | bytes 2097152 | tf_op jit(solution)/shard_map/psum | solution.py:107
  9.2 71.3 %collective-permute-start = (f32[4,128,128]{2,1,0:T(8,128)}, f32[4,128,128]{2,1,0:T(8,128)S(1)}, u32[]{:S(2)}, u32[]{:S(2)}) collective-permute-start(f32[4,128,128]{2,1,0:T(8,128)} %get-tuple-element.402), channel_id=1, source_target_pairs={{1,0},{2,1},{3,2},{4,3},{5,4},{6,5},{7,6},{8,7},{9,8},{10,9},{11,1... | collective-permute-start | bytes 786440 | tf_op jit(solution)/shard_map/ppermute | solution.py:23
  10.5 70.0 %collective-permute-start.1 = (f32[4,128,128]{2,1,0:T(8,128)}, f32[4,128,128]{2,1,0:T(8,128)}, u32[]{:S(2)}, u32[]{:S(2)}) collective-permute-start(f32[4,128,128]{2,1,0:T(8,128)} %get-tuple-element.403), channel_id=1, source_target_pairs={{0,1},{1,2},{2,3},{3,4},{4,5},{5,6},{6,7},{7,8},{8,9},{9,10},{10,1... | collective-permute-start | bytes 786440 | tf_op jit(solution)/shard_map/ppermute | solution.py:21
  15.8 37.8 %collective-permute-start.2 = (f32[4,128,128]{2,1,0:T(8,128)S(1)}, f32[4,128,128]{2,1,0:T(8,128)S(1)}, u32[]{:S(2)}, u32[]{:S(2)}) collective-permute-start(f32[4,128,128]{2,1,0:T(8,128)S(1)} %get-tuple-element.368), channel_id=1, source_target_pairs={{1,0},{2,1},{3,2},{4,3},{5,4},{6,5},{7,6},{8,7},{9,8},{10,9},{11,1... | collective-permute-start | bytes 786440 | tf_op jit(solution)/shard_map/ppermute | solution.py:23
  17.1 36.5 %collective-permute-start.3 = (f32[4,128,128]{2,1,0:T(8,128)S(1)}, f32[4,128,128]{2,1,0:T(8,128)S(1)}, u32[]{:S(2)}, u32[]{:S(2)}) collective-permute-start(f32[4,128,128]{2,1,0:T(8,128)S(1)} %get-tuple-element.369), channel_id=1, source_target_pairs={{0,1},{1,2},{2,3},{3,4},{4,5},{5,6},{6,7},{7,8},{8,9},{9,10},{10,1... | collective-permute-start | bytes 786440 | tf_op jit(solution)/shard_map/ppermute | solution.py:21
  76.1 13.6 %collective-permute-start.5 = (f32[4,128,128]{2,1,0:T(8,128)}, f32[4,128,128]{2,1,0:T(8,128)S(1)}, u32[]{:S(2)}, u32[]{:S(2)}) collective-permute-start(f32[4,128,128]{2,1,0:T(8,128)} %bitcast.18), channel_id=1, source_target_pairs={{0,1},{1,2},{2,3},{3,4},{4,5},{5,6},{6,7},{7,8},{8,9},{9,10},{10,1... | collective-permute-start | bytes 786440 | tf_op jit(solution)/shard_map/ppermute | solution.py:21
  78.0 17.2 %collective-permute-start.4 = (f32[4,128,128]{2,1,0:T(8,128)}, f32[4,128,128]{2,1,0:T(8,128)S(1)}, u32[]{:S(2)}, u32[]{:S(2)}) collective-permute-start(f32[4,128,128]{2,1,0:T(8,128)} %bitcast.17), channel_id=1, source_target_pairs={{1,0},{2,1},{3,2},{4,3},{5,4},{6,5},{7,6},{8,7},{9,8},{10,9},{11,1... | collective-permute-start | bytes 786440 | tf_op jit(solution)/shard_map/ppermute | solution.py:23
  104.7 9.2 %collective-permute-start.7 = (f32[4,128,128]{2,1,0:T(8,128)S(1)}, f32[4,128,128]{2,1,0:T(8,128)S(1)}, u32[]{:S(2)}, u32[]{:S(2)}) collective-permute-start(f32[4,128,128]{2,1,0:T(8,128)S(1)} %bitcast.291), channel_id=1, source_target_pairs={{0,1},{1,2},{2,3},{3,4},{4,5},{5,6},{6,7},{7,8},{8,9},{9,10},{10,1... | collective-permute-start | bytes 786440 | tf_op jit(solution)/shard_map/ppermute | solution.py:21
  108.6 15.3 %collective-permute-start.6 = (f32[4,128,128]{2,1,0:T(8,128)S(1)}, f32[4,128,128]{2,1,0:T(8,128)S(1)}, u32[]{:S(2)}, u32[]{:S(2)}) collective-permute-start(f32[4,128,128]{2,1,0:T(8,128)S(1)} %bitcast.278), channel_id=1, source_target_pairs={{1,0},{2,1},{3,2},{4,3},{5,4},{6,5},{7,6},{8,7},{9,8},{10,9},{11,1... | collective-permute-start | bytes 786440 | tf_op jit(solution)/shard_map/ppermute | solution.py:23
  135.2 9.0 %collective-permute-start.9 = (f32[4,128,128]{2,1,0:T(8,128)S(1)}, f32[4,128,128]{2,1,0:T(8,128)S(1)}, u32[]{:S(2)}, u32[]{:S(2)}) collective-permute-start(f32[4,128,128]{2,1,0:T(8,128)S(1)} %bitcast.292), channel_id=1, source_target_pairs={{0,1},{1,2},{2,3},{3,4},{4,5},{5,6},{6,7},{7,8},{8,9},{9,10},{10,1... | collective-permute-start | bytes 786440 | tf_op jit(solution)/shard_map/ppermute | solution.py:21
  138.9 15.1 %collective-permute-start.8 = (f32[4,128,128]{2,1,0:T(8,128)S(1)}, f32[4,128,128]{2,1,0:T(8,128)S(1)}, u32[]{:S(2)}, u32[]{:S(2)}) collective-permute-start(f32[4,128,128]{2,1,0:T(8,128)S(1)} %bitcast.279), channel_id=1, source_target_pairs={{1,0},{2,1},{3,2},{4,3},{5,4},{6,5},{7,6},{8,7},{9,8},{10,9},{11,1... | collective-permute-start | bytes 786440 | tf_op jit(solution)/shard_map/ppermute | solution.py:23
  163.3 8.0 %collective-permute-start.11 = (f32[4,128,128]{2,1,0:T(8,128)S(1)}, f32[4,128,128]{2,1,0:T(8,128)S(1)}, u32[]{:S(2)}, u32[]{:S(2)}) collective-permute-start(f32[4,128,128]{2,1,0:T(8,128)S(1)} %bitcast.293), channel_id=1, source_target_pairs={{0,1},{1,2},{2,3},{3,4},{4,5},{5,6},{6,7},{7,8},{8,9},{9,10},{10,1... | collective-permute-start | bytes 786440 | tf_op jit(solution)/shard_map/ppermute | solution.py:21
  165.7 15.5 %collective-permute-start.10 = (f32[4,128,128]{2,1,0:T(8,128)S(1)}, f32[4,128,128]{2,1,0:T(8,128)S(1)}, u32[]{:S(2)}, u32[]{:S(2)}) collective-permute-start(f32[4,128,128]{2,1,0:T(8,128)S(1)} %bitcast.280), channel_id=1, source_target_pairs={{1,0},{2,1},{3,2},{4,3},{5,4},{6,5},{7,6},{8,7},{9,8},{10,9},{11,1... | collective-permute-start | bytes 786440 | tf_op jit(solution)/shard_map/ppermute | solution.py:23
  214.8 10.2 %collective-permute-start.12 = (f32[4,128,128]{2,1,0:T(8,128)S(1)}, f32[4,128,128]{2,1,0:T(8,128)S(1)}, u32[]{:S(2)}, u32[]{:S(2)}) collective-permute-start(f32[4,128,128]{2,1,0:T(8,128)S(1)} %bitcast.281), channel_id=1, source_target_pairs={{1,0},{2,1},{3,2},{4,3},{5,4},{6,5},{7,6},{8,7},{9,8},{10,9},{11,1... | collective-permute-start | bytes 786440 | tf_op jit(solution)/shard_map/ppermute | solution.py:23
  236.7 7.0 collective-permute-start.15
  239.2 10.5 %collective-permute-start.14 = (f32[4,128,128]{2,1,0:T(8,128)S(1)}, f32[4,128,128]{2,1,0:T(8,128)S(1)}, u32[]{:S(2)}, u32[]{:S(2)}) collective-permute-start(f32[4,128,128]{2,1,0:T(8,128)S(1)} %bitcast.282), channel_id=1, source_target_pairs={{1,0},{2,1},{3,2},{4,3},{5,4},{6,5},{7,6},{8,7},{9,8},{10,9},{11,1... | collective-permute-start | bytes 786440 | tf_op jit(solution)/shard_map/ppermute | solution.py:23
  261.4 11.0 %collective-permute-start.16 = (f32[4,128,128]{2,1,0:T(8,128)S(1)}, f32[4,128,128]{2,1,0:T(8,128)S(1)}, u32[]{:S(2)}, u32[]{:S(2)}) collective-permute-start(f32[4,128,128]{2,1,0:T(8,128)S(1)} %bitcast.283), channel_id=1, source_target_pairs={{1,0},{2,1},{3,2},{4,3},{5,4},{6,5},{7,6},{8,7},{9,8},{10,9},{11,1... | collective-permute-start | bytes 786440 | tf_op jit(solution)/shard_map/ppermute | solution.py:23
  296.4 9.6 %collective-permute-start.18 = (f32[4,128,128]{2,1,0:T(8,128)S(1)}, f32[4,128,128]{2,1,0:T(8,128)S(1)}, u32[]{:S(2)}, u32[]{:S(2)}) collective-permute-start(f32[4,128,128]{2,1,0:T(8,128)S(1)} %bitcast.284), channel_id=1, source_target_pairs={{1,0},{2,1},{3,2},{4,3},{5,4},{6,5},{7,6},{8,7},{9,8},{10,9},{11,1... | collective-permute-start | bytes 786440 | tf_op jit(solution)/shard_map/ppermute | solution.py:23
  316.5 10.4 %collective-permute-start.20 = (f32[4,128,128]{2,1,0:T(8,128)S(1)}, f32[4,128,128]{2,1,0:T(8,128)S(1)}, u32[]{:S(2)}, u32[]{:S(2)}) collective-permute-start(f32[4,128,128]{2,1,0:T(8,128)S(1)} %bitcast.285), channel_id=1, source_target_pairs={{1,0},{2,1},{3,2},{4,3},{5,4},{6,5},{7,6},{8,7},{9,8},{10,9},{11,1... | collective-permute-start | bytes 786440 | tf_op jit(solution)/shard_map/ppermute | solution.py:23
  337.4 10.9 %collective-permute-start.22 = (f32[4,128,128]{2,1,0:T(8,128)S(1)}, f32[4,128,128]{2,1,0:T(8,128)S(1)}, u32[]{:S(2)}, u32[]{:S(2)}) collective-permute-start(f32[4,128,128]{2,1,0:T(8,128)S(1)} %bitcast.286), channel_id=1, source_target_pairs={{1,0},{2,1},{3,2},{4,3},{5,4},{6,5},{7,6},{8,7},{9,8},{10,9},{11,1... | collective-permute-start | bytes 786440 | tf_op jit(solution)/shard_map/ppermute | solution.py:23
  362.7 11.2 %collective-permute-start.24 = (f32[4,128,128]{2,1,0:T(8,128)S(1)}, f32[4,128,128]{2,1,0:T(8,128)}, u32[]{:S(2)}, u32[]{:S(2)}) collective-permute-start(f32[4,128,128]{2,1,0:T(8,128)S(1)} %bitcast.287), channel_id=1, source_target_pairs={{1,0},{2,1},{3,2},{4,3},{5,4},{6,5},{7,6},{8,7},{9,8},{10,9},{11,1... | collective-permute-start | bytes 786440 | tf_op jit(solution)/shard_map/ppermute | solution.py:23
  389.5 11.2 %collective-permute-start.26 = (f32[4,128,128]{2,1,0:T(8,128)S(1)}, f32[4,128,128]{2,1,0:T(8,128)}, u32[]{:S(2)}, u32[]{:S(2)}) collective-permute-start(f32[4,128,128]{2,1,0:T(8,128)S(1)} %bitcast.288), channel_id=1, source_target_pairs={{1,0},{2,1},{3,2},{4,3},{5,4},{6,5},{7,6},{8,7},{9,8},{10,9},{11,1... | collective-permute-start | bytes 786440 | tf_op jit(solution)/shard_map/ppermute | solution.py:23
  416.5 11.2 %collective-permute-start.28 = (f32[4,128,128]{2,1,0:T(8,128)S(1)}, f32[4,128,128]{2,1,0:T(8,128)}, u32[]{:S(2)}, u32[]{:S(2)}) collective-permute-start(f32[4,128,128]{2,1,0:T(8,128)S(1)} %bitcast.289), channel_id=1, source_target_pairs={{1,0},{2,1},{3,2},{4,3},{5,4},{6,5},{7,6},{8,7},{9,8},{10,9},{11,1... | collective-permute-start | bytes 786440 | tf_op jit(solution)/shard_map/ppermute | solution.py:23
  443.5 11.2 %collective-permute-start.30 = (f32[4,128,128]{2,1,0:T(8,128)S(1)}, f32[4,128,128]{2,1,0:T(8,128)}, u32[]{:S(2)}, u32[]{:S(2)}) collective-permute-start(f32[4,128,128]{2,1,0:T(8,128)S(1)} %bitcast.290), channel_id=1, source_target_pairs={{1,0},{2,1},{3,2},{4,3},{5,4},{6,5},{7,6},{8,7},{9,8},{10,9},{11,1... | collective-permute-start | bytes 786440 | tf_op jit(solution)/shard_map/ppermute | solution.py:23
  (58 other events, 776.4 us)
Sparse Core Ops, SparseCore 0:
  472.9 176.9 all-reduce.257
where the time goes:
time: 713 us; the launch traced here: 705 us
  waiting for transfers between devices  301 us (42%)
  other arithmetic  139 us (19%)
  local copies, waits for them, and re-layouts  131 us (18%)
  starting transfers between devices  68.4 us (10%)
  blocking collectives  43.5 us (6%)
  between operations  22.2 us (3%)
    psum x1, waiting for transfers between devices, on_device(): total = lax.psum(gradient, 'shot')  177 us
    ppermute x16, waiting for transfers between devices, padded_2(): lax.ppermute(head, axis, [((i + 1) % count, i) for i in range(ends)])  97.7 us
    slice x128, local copies, waits for them, and re-layouts, shifted(): lax.slice_in_dim(field, offset, length, axis=axis)  88.1 us
    add x8, other arithmetic, on_device(): newer = 2.0 * current - older + model_slab * image  51.9 us
    ppermute x16, starting transfers between devices, padded_2(): lax.ppermute(tail, axis, [(i, (i + 1) % count) for i in range(ends)])  44 us
    pmax x1, blocking collectives, on_device(): peak = lax.pmax(jnp.max(jnp.abs(total)), 'dom')  43.5 us
    add x8, other arithmetic, on_device(): earlier = 2.0 * present - later + model_slab * laplace(padded)  41.5 us
    scatter-add x16, other arithmetic, add_at(): return field.reshape(-1).at[slots].add(values).reshape(field.shape)  34.6 us
  transfers between devices with their start and end apart: 33, of which 28 were waited for; matrix products, arithmetic and copies ran while one was open for 10% of the time, Pallas kernels for 0%

commit v1 on v0

--- a/solution.py
+++ b/solution.py
@@ -104,7 +104,7 @@
         earlier = add_at(earlier, own_row, receivers, residuals[tick])
         gradient = gradient + earlier * images[tick]
         later, present = (present, earlier)
-    total = lax.psum(gradient, "shot")
+    total = jnp.sum(lax.all_gather(gradient, "shot"), axis=0)
     peak = lax.pmax(jnp.max(jnp.abs(total)), "dom")
     direction = total / (peak + EPSILON)
     new_model = model_slab * (1.0 - STEP_FRACTION * direction)

time: 713 us -> 717 us (level)
    psum x1 -> x0, waiting for transfers between devices: 177 us -> none  [on_device(): total = lax.psum(gradient, 'shot')]
    all_gather x0 -> x1, waiting for transfers between devices: none -> 171 us  [on_device(): total = jnp.sum(lax.all_gather(gradient, 'shot'), axis=0)]
    reduce_sum x0 -> x1, other arithmetic: none -> 7.44 us  [on_device(): total = jnp.sum(lax.all_gather(gradient, 'shot'), axis=0)]
where the time goes in v1:
time: 717 us; the launch traced here: 707 us
  waiting for transfers between devices  300 us (42%)
  other arithmetic  146 us (20%)
  local copies, waits for them, and re-layouts  133 us (19%)
  starting transfers between devices  67.7 us (9%)
  blocking collectives  38.6 us (5%)
  between operations  22.1 us (3%)
    all_gather x1, waiting for transfers between devices, on_device(): total = jnp.sum(lax.all_gather(gradient, 'shot'), axis=0)  171 us
    ppermute x16, waiting for transfers between devices, padded_2(): lax.ppermute(head, axis, [((i + 1) % count, i) for i in range(ends)])  96.9 us
    slice x128, local copies, waits for them, and re-layouts, shifted(): lax.slice_in_dim(field, offset, length, axis=axis)  83.1 us
    add x8, other arithmetic, on_device(): newer = 2.0 * current - older + model_slab * image  52.7 us
    ppermute x16, starting transfers between devices, padded_2(): lax.ppermute(tail, axis, [(i, (i + 1) % count) for i in range(ends)])  43.7 us
    add x8, other arithmetic, on_device(): earlier = 2.0 * present - later + model_slab * laplace(padded)  39.4 us
    pmax x1, blocking collectives, on_device(): peak = lax.pmax(jnp.max(jnp.abs(total)), 'dom')  38.6 us
    gather x8, local copies, waits for them, and re-layouts, on_device(): values = newer.reshape(-1)[receiver_slots] - observed[0, tick]  35.3 us
  transfers between devices with their start and end apart: 33, of which 28 were waited for; matrix products, arithmetic and copies ran while one was open for 10% of the time, Pallas kernels for 0%

profile of v1, /device:TPU:0, one launch (start us, length us, event | category | flops | bytes accessed | tf_op | source)
XLA Modules:
  0.0 706.8 jit_solution(5551761561673974648)
XLA Ops:
  55.1 9.5 %fusion.432 = (f32[16,128,128]{2,1,0:T(8,128)S(1)}, f32[16,128,128]{2,1,0:T(8,128)}) fusion(f32[1,16,128,128]{3,2,1,0:T(8,128)} %param.26, f32[16,128,128]{2,1,0:T(8,128)} %param.25, f32[1,16,128,128]{3,2,1,0:T(8,128)S(1)} %copy-done.9, f32[16,128,124]{2,1,0:T(8,128)} %get-tuple-element.385, f32[16,128,124]{2,1,0:T(8,128)} %get-tuple-element.384, ...), kind=kLoop, calls=%fused_computation.673 | loop fusion | flops 12845056 | bytes 23265280 | tf_op jit(solution)/shard_map/add | solution.py:94
  82.3 7.3 %fusion.388 = f32[16,128,128]{2,1,0:T(8,128)S(1)} fusion(f32[16,128,128]{2,1,0:T(8,128)S(1)} %copy-done.13, f32[16,128,128]{2,1,0:T(8,128)S(1)} %bitcast.276, f32[4,128,128]{2,1,0:T(8,128)} %collective-permute-done.1, f32[4,128,128]{2,1,0:T(8,128)S(1)} %collective-permute-done, f32[1,16,128,128]{3,2,1,0:T(8,128)} %param.28, ...), kind=kLoop, calls=%fused_computation.596 | loop fusion | flops 12845056 | bytes 21168128 | tf_op jit(solution)/shard_map/add | solution.py:103
  90.9 5.7 collective-permute-done.4
  115.9 9.9 %collective-permute-done.6 = f32[4,128,128]{2,1,0:T(8,128)S(1)} collective-permute-done((f32[4,128,128]{2,1,0:T(8,128)S(1)}, f32[4,128,128]{2,1,0:T(8,128)S(1)}, u32[]{:S(2)}, u32[]{:S(2)}) %collective-permute-start.6) | collective-permute-done | bytes 262176 | tf_op jit(solution)/shard_map/ppermute | solution.py:23
  126.5 7.5 %multiply_add_fusion.6 = (f32[16,128,128]{2,1,0:T(8,128)S(1)}, f32[16,128,128]{2,1,0:T(8,128)}) fusion(f32[16,128,128]{2,1,0:T(8,128)S(1)} %copy-done.14, f32[16,128,128]{2,1,0:T(8,128)S(1)} %bitcast.226, f32[16,128,128]{2,1,0:T(8,128)} %bitcast.236, f32[16,128,124]{2,1,0:T(8,128)S(1)} %get-tuple-element.349, f32[16,128,124]{2,1,0:T(8,128)S(1)} %get-tuple-element.348, ...), kind=kLoop, calls=%fused_computation.683 | loop fusion | flops 12845056 | bytes 22216704 | tf_op jit(solution)/shard_map/add | solution.py:94
  146.9 9.8 %collective-permute-done.8 = f32[4,128,128]{2,1,0:T(8,128)S(1)} collective-permute-done((f32[4,128,128]{2,1,0:T(8,128)S(1)}, f32[4,128,128]{2,1,0:T(8,128)S(1)}, u32[]{:S(2)}, u32[]{:S(2)}) %collective-permute-start.8) | collective-permute-done | bytes 262176 | tf_op jit(solution)/shard_map/ppermute | solution.py:23
  175.2 10.7 %collective-permute-done.10 = f32[4,128,128]{2,1,0:T(8,128)} collective-permute-done((f32[4,128,128]{2,1,0:T(8,128)S(1)}, f32[4,128,128]{2,1,0:T(8,128)}, u32[]{:S(2)}, u32[]{:S(2)}) %collective-permute-start.10) | collective-permute-done | bytes 262176 | tf_op jit(solution)/shard_map/ppermute | solution.py:23
  185.9 5.7 multiply_add_fusion.4
  193.1 10.9 %gather_fusion.3 = f32[256]{0:T(256)} fusion(f32[262144]{0:T(1024)} %fusion.437, s32[1024]{0:T(1024)S(1)} %pad_clamp_fusion), kind=kCustom, calls=%fused_computation.3 | custom fusion | bytes 3072 | tf_op jit(solution)/shard_map/gather | solution.py:96
  231.7 7.7 %multiply_add_fusion.3 = (f32[16,128,128]{2,1,0:T(8,128)S(1)}, f32[16,128,128]{2,1,0:T(8,128)}) fusion(f32[16,128,128]{2,1,0:T(8,128)S(1)} %copy-done.17, f32[16,128,128]{2,1,0:T(8,128)S(1)} %bitcast.204, f32[16,128,128]{2,1,0:T(8,128)} %bitcast.40, f32[16,128,124]{2,1,0:T(8,128)S(1)} %get-tuple-element.295, f32[16,128,124]{2,1,0:T(8,128)S(1)} %get-tuple-element.294, ...), kind=kLoop, calls=%fused_computation.680 | loop fusion | flops 12845056 | bytes 22216704 | tf_op jit(solution)/shard_map/add | solution.py:94
  251.0 5.8 collective-permute-done.14
  274.5 6.7 collective-permute-done.16
  281.2 5.6 multiply_add_fusion.1
  288.3 10.4 %gather_fusion = f32[256]{0:T(256)S(1)} fusion(f32[262144]{0:T(1024)} %fusion.440, s32[1024]{0:T(1024)S(1)} %pad_clamp_fusion), kind=kCustom, calls=%fused_computation | custom fusion | bytes 3072 | tf_op jit(solution)/shard_map/gather | solution.py:96
  330.2 6.0 collective-permute-done.20
  351.3 6.2 collective-permute-done.22
  376.6 6.3 collective-permute-done.24
  402.0 6.4 collective-permute-done.26
  428.6 6.5 collective-permute-done.28
  455.3 6.4 collective-permute-done.30
  471.6 7.8 %multiply_add_fusion = f32[16,128,128]{2,1,0:T(8,128)} fusion(f32[16,128,128]{2,1,0:T(8,128)} %bitcast.279, f32[16,128,128]{2,1,0:T(8,128)} %get-tuple-element.115, f32[16,128,128]{2,1,0:T(8,128)} %bitcast.239, f32[16,128,128]{2,1,0:T(8,128)} %get-tuple-element.113, f32[16,128,128]{2,1,0:T(8,128)} %bitcast.172, f32[16,128,128]{2,1,0:T(8,128)} %get-tuple-element.111, ...), kind=kLoop, calls=%fused_computation.677 | loop fusion | flops 3932160 | bytes 17825792 | tf_op jit(solution)/shard_map/add | solution.py:105
  479.5 171.3 %all-gather.3.cloned.1.call-done = f32[256,128,128]{2,1,0:T(8,128)} async-done(((f32[16,128,128]{2,1,0:T(8,128)}), f32[256,128,128]{2,1,0:T(8,128)}) %all-gather.3.cloned.1.call-update) | async-done | bytes 16777232 | tf_op jit(solution)/shard_map/all_gather | solution.py:107
  650.7 7.4 %reduce_sum.9 = f32[16,128,128]{2,1,0:T(8,128)S(1)} reduce(f32[16,16,128,128]{3,2,1,0:T(8,128)} %bitcast.277, f32[]{:T(128)} %constant.180.clone.1), dimensions={0}, to_apply=%region_8.9 | reduce | flops 3932160 | bytes 17825796 | tf_op jit(solution)/shard_map/reduce_sum | solution.py:107
  658.9 38.6 %pmax.7 = f32[]{:T(128)} all-reduce(f32[]{:T(128)} %abs_reduce_fusion), channel_id=1, replica_groups=mesh['shot'=16,'dom'=16] {'dom'}, use_global_device_ids=true, to_apply=%region_10.11 | all-reduce | flops 1 | bytes 8 | tf_op jit(solution)/shard_map/pmax | solution.py:108
  (350 shorter events, 308.6 us)
Async XLA Ops:
  7.2 643.5 %all-gather.3.cloned.1.call-start = ((), (), s32[]{:S(2)}) async-start(), calls=%async_computation | async-start | bytes 17825792 | tf_op jit(solution)/shard_map/all_gather | solution.py:107
  9.2 72.9 %collective-permute-start = (f32[4,128,128]{2,1,0:T(8,128)}, f32[4,128,128]{2,1,0:T(8,128)S(1)}, u32[]{:S(2)}, u32[]{:S(2)}) collective-permute-start(f32[4,128,128]{2,1,0:T(8,128)} %get-tuple-element.402), channel_id=1, source_target_pairs={{1,0},{2,1},{3,2},{4,3},{5,4},{6,5},{7,6},{8,7},{9,8},{10,9},{11,1... | collective-permute-start | bytes 786440 | tf_op jit(solution)/shard_map/ppermute | solution.py:23
  10.5 71.6 %collective-permute-start.1 = (f32[4,128,128]{2,1,0:T(8,128)}, f32[4,128,128]{2,1,0:T(8,128)}, u32[]{:S(2)}, u32[]{:S(2)}) collective-permute-start(f32[4,128,128]{2,1,0:T(8,128)} %get-tuple-element.403), channel_id=1, source_target_pairs={{0,1},{1,2},{2,3},{3,4},{4,5},{5,6},{6,7},{7,8},{8,9},{9,10},{10,1... | collective-permute-start | bytes 786440 | tf_op jit(solution)/shard_map/ppermute | solution.py:21
  15.9 38.5 %collective-permute-start.2 = (f32[4,128,128]{2,1,0:T(8,128)S(1)}, f32[4,128,128]{2,1,0:T(8,128)S(1)}, u32[]{:S(2)}, u32[]{:S(2)}) collective-permute-start(f32[4,128,128]{2,1,0:T(8,128)S(1)} %get-tuple-element.368), channel_id=1, source_target_pairs={{1,0},{2,1},{3,2},{4,3},{5,4},{6,5},{7,6},{8,7},{9,8},{10,9},{11,1... | collective-permute-start | bytes 786440 | tf_op jit(solution)/shard_map/ppermute | solution.py:23
  17.2 37.2 %collective-permute-start.3 = (f32[4,128,128]{2,1,0:T(8,128)S(1)}, f32[4,128,128]{2,1,0:T(8,128)S(1)}, u32[]{:S(2)}, u32[]{:S(2)}) collective-permute-start(f32[4,128,128]{2,1,0:T(8,128)S(1)} %get-tuple-element.369), channel_id=1, source_target_pairs={{0,1},{1,2},{2,3},{3,4},{4,5},{5,6},{6,7},{7,8},{8,9},{9,10},{10,1... | collective-permute-start | bytes 786440 | tf_op jit(solution)/shard_map/ppermute | solution.py:21
  77.4 13.5 %collective-permute-start.5 = (f32[4,128,128]{2,1,0:T(8,128)}, f32[4,128,128]{2,1,0:T(8,128)}, u32[]{:S(2)}, u32[]{:S(2)}) collective-permute-start(f32[4,128,128]{2,1,0:T(8,128)} %bitcast.18), channel_id=1, source_target_pairs={{0,1},{1,2},{2,3},{3,4},{4,5},{5,6},{6,7},{7,8},{8,9},{9,10},{10,1... | collective-permute-start | bytes 786440 | tf_op jit(solution)/shard_map/ppermute | solution.py:21
  80.0 16.6 %collective-permute-start.4 = (f32[4,128,128]{2,1,0:T(8,128)}, f32[4,128,128]{2,1,0:T(8,128)}, u32[]{:S(2)}, u32[]{:S(2)}) collective-permute-start(f32[4,128,128]{2,1,0:T(8,128)} %bitcast.17), channel_id=1, source_target_pairs={{1,0},{2,1},{3,2},{4,3},{5,4},{6,5},{7,6},{8,7},{9,8},{10,9},{11,1... | collective-permute-start | bytes 786440 | tf_op jit(solution)/shard_map/ppermute | solution.py:23
  106.7 9.2 %collective-permute-start.7 = (f32[4,128,128]{2,1,0:T(8,128)S(1)}, f32[4,128,128]{2,1,0:T(8,128)S(1)}, u32[]{:S(2)}, u32[]{:S(2)}) collective-permute-start(f32[4,128,128]{2,1,0:T(8,128)S(1)} %bitcast.293), channel_id=1, source_target_pairs={{0,1},{1,2},{2,3},{3,4},{4,5},{5,6},{6,7},{7,8},{8,9},{9,10},{10,1... | collective-permute-start | bytes 786440 | tf_op jit(solution)/shard_map/ppermute | solution.py:21
  110.7 15.2 %collective-permute-start.6 = (f32[4,128,128]{2,1,0:T(8,128)S(1)}, f32[4,128,128]{2,1,0:T(8,128)S(1)}, u32[]{:S(2)}, u32[]{:S(2)}) collective-permute-start(f32[4,128,128]{2,1,0:T(8,128)S(1)} %bitcast.280), channel_id=1, source_target_pairs={{1,0},{2,1},{3,2},{4,3},{5,4},{6,5},{7,6},{8,7},{9,8},{10,9},{11,1... | collective-permute-start | bytes 786440 | tf_op jit(solution)/shard_map/ppermute | solution.py:23
  138.6 8.3 %collective-permute-start.9 = (f32[4,128,128]{2,1,0:T(8,128)S(1)}, f32[4,128,128]{2,1,0:T(8,128)S(1)}, u32[]{:S(2)}, u32[]{:S(2)}) collective-permute-start(f32[4,128,128]{2,1,0:T(8,128)S(1)} %bitcast.294), channel_id=1, source_target_pairs={{0,1},{1,2},{2,3},{3,4},{4,5},{5,6},{6,7},{7,8},{8,9},{9,10},{10,1... | collective-permute-start | bytes 786440 | tf_op jit(solution)/shard_map/ppermute | solution.py:21
  141.5 15.1 %collective-permute-start.8 = (f32[4,128,128]{2,1,0:T(8,128)S(1)}, f32[4,128,128]{2,1,0:T(8,128)S(1)}, u32[]{:S(2)}, u32[]{:S(2)}) collective-permute-start(f32[4,128,128]{2,1,0:T(8,128)S(1)} %bitcast.281), channel_id=1, source_target_pairs={{1,0},{2,1},{3,2},{4,3},{5,4},{6,5},{7,6},{8,7},{9,8},{10,9},{11,1... | collective-permute-start | bytes 786440 | tf_op jit(solution)/shard_map/ppermute | solution.py:23
  167.3 8.0 %collective-permute-start.11 = (f32[4,128,128]{2,1,0:T(8,128)S(1)}, f32[4,128,128]{2,1,0:T(8,128)}, u32[]{:S(2)}, u32[]{:S(2)}) collective-permute-start(f32[4,128,128]{2,1,0:T(8,128)S(1)} %bitcast.295), channel_id=1, source_target_pairs={{0,1},{1,2},{2,3},{3,4},{4,5},{5,6},{6,7},{7,8},{8,9},{9,10},{10,1... | collective-permute-start | bytes 786440 | tf_op jit(solution)/shard_map/ppermute | solution.py:21
  170.3 15.6 %collective-permute-start.10 = (f32[4,128,128]{2,1,0:T(8,128)S(1)}, f32[4,128,128]{2,1,0:T(8,128)}, u32[]{:S(2)}, u32[]{:S(2)}) collective-permute-start(f32[4,128,128]{2,1,0:T(8,128)S(1)} %bitcast.282), channel_id=1, source_target_pairs={{1,0},{2,1},{3,2},{4,3},{5,4},{6,5},{7,6},{8,7},{9,8},{10,9},{11,1... | collective-permute-start | bytes 786440 | tf_op jit(solution)/shard_map/ppermute | solution.py:23
  218.8 7.0 collective-permute-start.13
  220.1 10.8 %collective-permute-start.12 = (f32[4,128,128]{2,1,0:T(8,128)S(1)}, f32[4,128,128]{2,1,0:T(8,128)S(1)}, u32[]{:S(2)}, u32[]{:S(2)}) collective-permute-start(f32[4,128,128]{2,1,0:T(8,128)S(1)} %bitcast.283), channel_id=1, source_target_pairs={{1,0},{2,1},{3,2},{4,3},{5,4},{6,5},{7,6},{8,7},{9,8},{10,9},{11,1... | collective-permute-start | bytes 786440 | tf_op jit(solution)/shard_map/ppermute | solution.py:23
  246.2 10.6 %collective-permute-start.14 = (f32[4,128,128]{2,1,0:T(8,128)S(1)}, f32[4,128,128]{2,1,0:T(8,128)S(1)}, u32[]{:S(2)}, u32[]{:S(2)}) collective-permute-start(f32[4,128,128]{2,1,0:T(8,128)S(1)} %bitcast.284), channel_id=1, source_target_pairs={{1,0},{2,1},{3,2},{4,3},{5,4},{6,5},{7,6},{8,7},{9,8},{10,9},{11,1... | collective-permute-start | bytes 786440 | tf_op jit(solution)/shard_map/ppermute | solution.py:23
  270.5 10.7 %collective-permute-start.16 = (f32[4,128,128]{2,1,0:T(8,128)S(1)}, f32[4,128,128]{2,1,0:T(8,128)}, u32[]{:S(2)}, u32[]{:S(2)}) collective-permute-start(f32[4,128,128]{2,1,0:T(8,128)S(1)} %bitcast.285), channel_id=1, source_target_pairs={{1,0},{2,1},{3,2},{4,3},{5,4},{6,5},{7,6},{8,7},{9,8},{10,9},{11,1... | collective-permute-start | bytes 786440 | tf_op jit(solution)/shard_map/ppermute | solution.py:23
  305.7 9.7 %collective-permute-start.18 = (f32[4,128,128]{2,1,0:T(8,128)S(1)}, f32[4,128,128]{2,1,0:T(8,128)S(1)}, u32[]{:S(2)}, u32[]{:S(2)}) collective-permute-start(f32[4,128,128]{2,1,0:T(8,128)S(1)} %bitcast.286), channel_id=1, source_target_pairs={{1,0},{2,1},{3,2},{4,3},{5,4},{6,5},{7,6},{8,7},{9,8},{10,9},{11,1... | collective-permute-start | bytes 786440 | tf_op jit(solution)/shard_map/ppermute | solution.py:23
  325.9 10.3 %collective-permute-start.20 = (f32[4,128,128]{2,1,0:T(8,128)S(1)}, f32[4,128,128]{2,1,0:T(8,128)S(1)}, u32[]{:S(2)}, u32[]{:S(2)}) collective-permute-start(f32[4,128,128]{2,1,0:T(8,128)S(1)} %bitcast.287), channel_id=1, source_target_pairs={{1,0},{2,1},{3,2},{4,3},{5,4},{6,5},{7,6},{8,7},{9,8},{10,9},{11,1... | collective-permute-start | bytes 786440 | tf_op jit(solution)/shard_map/ppermute | solution.py:23
  346.8 10.7 %collective-permute-start.22 = (f32[4,128,128]{2,1,0:T(8,128)S(1)}, f32[4,128,128]{2,1,0:T(8,128)S(1)}, u32[]{:S(2)}, u32[]{:S(2)}) collective-permute-start(f32[4,128,128]{2,1,0:T(8,128)S(1)} %bitcast.288), channel_id=1, source_target_pairs={{1,0},{2,1},{3,2},{4,3},{5,4},{6,5},{7,6},{8,7},{9,8},{10,9},{11,1... | collective-permute-start | bytes 786440 | tf_op jit(solution)/shard_map/ppermute | solution.py:23
  372.0 11.0 %collective-permute-start.24 = (f32[4,128,128]{2,1,0:T(8,128)S(1)}, f32[4,128,128]{2,1,0:T(8,128)S(1)}, u32[]{:S(2)}, u32[]{:S(2)}) collective-permute-start(f32[4,128,128]{2,1,0:T(8,128)S(1)} %bitcast.289), channel_id=1, source_target_pairs={{1,0},{2,1},{3,2},{4,3},{5,4},{6,5},{7,6},{8,7},{9,8},{10,9},{11,1... | collective-permute-start | bytes 786440 | tf_op jit(solution)/shard_map/ppermute | solution.py:23
  397.3 11.1 %collective-permute-start.26 = (f32[4,128,128]{2,1,0:T(8,128)S(1)}, f32[4,128,128]{2,1,0:T(8,128)S(1)}, u32[]{:S(2)}, u32[]{:S(2)}) collective-permute-start(f32[4,128,128]{2,1,0:T(8,128)S(1)} %bitcast.290), channel_id=1, source_target_pairs={{1,0},{2,1},{3,2},{4,3},{5,4},{6,5},{7,6},{8,7},{9,8},{10,9},{11,1... | collective-permute-start | bytes 786440 | tf_op jit(solution)/shard_map/ppermute | solution.py:23
  423.9 11.2 %collective-permute-start.28 = (f32[4,128,128]{2,1,0:T(8,128)S(1)}, f32[4,128,128]{2,1,0:T(8,128)S(1)}, u32[]{:S(2)}, u32[]{:S(2)}) collective-permute-start(f32[4,128,128]{2,1,0:T(8,128)S(1)} %bitcast.291), channel_id=1, source_target_pairs={{1,0},{2,1},{3,2},{4,3},{5,4},{6,5},{7,6},{8,7},{9,8},{10,9},{11,1... | collective-permute-start | bytes 786440 | tf_op jit(solution)/shard_map/ppermute | solution.py:23
  450.6 11.1 %collective-permute-start.30 = (f32[4,128,128]{2,1,0:T(8,128)S(1)}, f32[4,128,128]{2,1,0:T(8,128)S(1)}, u32[]{:S(2)}, u32[]{:S(2)}) collective-permute-start(f32[4,128,128]{2,1,0:T(8,128)S(1)} %bitcast.292), channel_id=1, source_target_pairs={{1,0},{2,1},{3,2},{4,3},{5,4},{6,5},{7,6},{8,7},{9,8},{10,9},{11,1... | collective-permute-start | bytes 786440 | tf_op jit(solution)/shard_map/ppermute | solution.py:23
  (65 other events, 581.6 us)
Sparse Core Ops, SparseCore 0:
  479.6 171.1 all-gather.2
